TPU v7x, 256 devices: a whole 4x4x8 slice. The times are simulated.
256 devices in a mesh: dp: 4 (over x), expert: 8 (over z), tensor: 8 (over y, core).
Axes of the slice: x: 4, y: 4, z: 8, core: 2. Of those that a mesh axis runs over, the one named last changes fastest.
Arguments:
- tokens: bfloat16 [1024, 6144], P('expert'), may hold values from -6 to 6
- routes: int32 [1024, 2], P('expert'), may hold values from 0 to 7, all different within a row; in each aligned block of 128 rows (0 to 127, 128 to 255, ...) at most 64 rows name the same one
- logits: float32 [1024, 2], P('expert'), may hold values from -8 to 8
- grad_out: bfloat16 [1024, 6144], P('expert'), may hold values from -6 to 6
- w_gate: bfloat16 [8, 6144, 8192], P('expert', None, ('dp', 'tensor')), may hold values from -0.078125 to 0.078125
- w_up: bfloat16 [8, 6144, 8192], P('expert', None, ('dp', 'tensor')), may hold values from -0.078125 to 0.078125
- w_down: bfloat16 [8, 8192, 6144], P('expert', ('dp', 'tensor')), may hold values from -0.0625 to 0.0625
Outputs:
- output: bfloat16 [1024, 6144], P(('expert', 'tensor'))
- grad_tokens: bfloat16 [1024, 6144], P(('expert', 'tensor'))
Inputs may be any that keep to these rules, and one draw needn't show every extreme that they name: `routes`: each token names two different experts. The 128 tokens of one index of the expert axis name one expert at most 64 times, and in every draw some expert is named exactly 64 times by the tokens of some index.
All inputs are finite; a program needn't handle non-finite values.
Results may differ from a plain program's by a relative error of at most 0.015.
Values may be sent and summed in bfloat16 or wider, within the bound.
No kernel may reach another device: no remote copies, remote signals or barrier semaphores. Data moves between devices by JAX's collectives and lax.ppermute only.
A program may use at most 128 MiB of HBM per device.

v0:
```python
import jax
import jax.numpy as jnp
from jax import lax
from jax.sharding import PartitionSpec as P


def slot_targets(routes, experts, capacity):
    flat = routes.reshape(-1)
    labels = jnp.arange(experts, dtype=jnp.int32)
    onehot = (flat[:, None] == labels[None, :]).astype(jnp.int32)
    before = jnp.cumsum(onehot, axis=0) - onehot
    slot = jnp.sum(before * onehot, axis=1)
    return (flat * capacity + slot).reshape(-1, 2)


def activate(gate, up):
    sig = jax.nn.sigmoid(gate)
    return (gate * sig * up).astype(jnp.bfloat16)


def backprop(grad_hidden, gate, up):
    sig = jax.nn.sigmoid(gate)
    grad_gate = (grad_hidden * up * sig * (1.0 + gate * (1.0 - sig))).astype(jnp.bfloat16)
    grad_up = (grad_hidden * gate * sig).astype(jnp.bfloat16)
    return (grad_gate, grad_up)


def local(tokens, routes, logits, grad_out, w_gate, w_up, w_down):
    experts = lax.axis_size("expert")
    lanes = lax.axis_size("dp")
    tensor_size = lax.axis_size("tensor")
    group = lanes * tensor_size
    count, width = tokens.shape
    capacity = 4 * count // experts
    gate_w = w_gate[0]
    up_w = w_up[0]
    down_w = w_down[0]
    inner = gate_w.shape[1]
    contract_last = (((1,), (1,)), ((), ()))
    target = slot_targets(routes, experts, capacity)
    share = jax.nn.sigmoid(logits[:, 0] - logits[:, 1])
    weight_one = share[:, None]
    weight_two = (1.0 - share)[:, None]
    grad_one = (weight_one * grad_out.astype(jnp.float32)).astype(jnp.bfloat16)
    grad_two = (weight_two * grad_out.astype(jnp.float32)).astype(jnp.bfloat16)

    def project_in(flat):
        gate = jnp.dot(flat, gate_w, preferred_element_type=jnp.float32)
        up = jnp.dot(flat, up_w, preferred_element_type=jnp.float32)
        return jnp.concatenate([gate, up], axis=1)

    def project_back(flat):
        return lax.dot_general(flat, down_w, contract_last, preferred_element_type=jnp.float32)

    portion = capacity // group
    offset = lax.axis_index(("dp", "tensor")) * portion
    places = (
        jnp.arange(experts, dtype=jnp.int32)[:, None] * capacity
        + offset
        + jnp.arange(portion, dtype=jnp.int32)[None, :]
    )
    build_places = places.reshape(-1)
    first = (build_places[:, None] == target[None, :, 0]).astype(jnp.bfloat16)
    second = (build_places[:, None] == target[None, :, 1]).astype(jnp.bfloat16)
    rows_fwd = jnp.dot(first + second, tokens, preferred_element_type=jnp.float32).astype(
        jnp.bfloat16
    )
    rows_bwd = jnp.dot(first, grad_one, preferred_element_type=jnp.float32)
    rows_bwd = (rows_bwd + jnp.dot(second, grad_two, preferred_element_type=jnp.float32)).astype(
        jnp.bfloat16
    )
    rows_fwd, rows_bwd = (rows_fwd, rows_bwd)
    shape = (experts, portion, width)
    got_fwd, got_bwd = (
        lax.all_to_all(rows_fwd.reshape(shape), "expert", split_axis=0, concat_axis=0, tiled=True),
        lax.all_to_all(rows_bwd.reshape(shape), "expert", split_axis=0, concat_axis=0, tiled=True),
    )

    def move_in(arrived, project):
        piece = lax.all_gather(arrived, ("dp", "tensor"), axis=1, tiled=True)
        result = project(piece.reshape(-1, width))
        spread = result.reshape(piece.shape[0], piece.shape[1], -1)
        return spread.reshape(-1, spread.shape[2])

    share_rows = count // tensor_size
    piece_rows = share_rows // lanes
    position = jnp.arange(count, dtype=jnp.int32)
    block_index = position // piece_rows
    within = position % piece_rows
    source = (
        block_index % tensor_size * share_rows + block_index // tensor_size * piece_rows + within
    )
    slot_one = target[source, 0]
    slot_two = target[source, 1]
    first_weight = weight_one[source]
    second_weight = weight_two[source]

    def settle(term, left_weight, right_weight):
        shaped = term.astype(jnp.bfloat16).reshape(experts, capacity, width)
        back = lax.all_to_all(shaped, "expert", split_axis=0, concat_axis=0, tiled=True).reshape(
            -1, width
        )
        mixed = left_weight * back[slot_one].astype(jnp.float32) + right_weight * back[
            slot_two
        ].astype(jnp.float32)
        mixed = lax.optimization_barrier(mixed.astype(jnp.bfloat16)).astype(jnp.float32)
        summed = lax.psum_scatter(
            mixed.astype(jnp.bfloat16), ("dp", "tensor"), scatter_dimension=0, tiled=True
        )
        return summed

    projected = move_in(got_fwd, project_in)
    gate = projected[:, :inner]
    up = projected[:, inner:]
    hidden = activate(gate, up)
    out_piece = settle(
        jnp.dot(hidden, down_w, preferred_element_type=jnp.float32), first_weight, second_weight
    )
    grad_hidden = move_in(got_bwd, project_back)
    grad_gate, grad_up = backprop(grad_hidden, gate, up)
    term = lax.dot_general(grad_gate, gate_w, contract_last, preferred_element_type=jnp.float32)
    term = term + lax.dot_general(grad_up, up_w, contract_last, preferred_element_type=jnp.float32)
    grad_piece = settle(term, 1.0, 1.0)
    output, grad_tokens = (
        lax.all_gather(out_piece, "dp", axis=0, tiled=True),
        lax.all_gather(grad_piece, "dp", axis=0, tiled=True),
    )
    return (output, grad_tokens)


def solution(mesh):
    return jax.shard_map(
        local,
        mesh=mesh,
        in_specs=(
            P("expert", None),
            P("expert", None),
            P("expert", None),
            P("expert", None),
            P("expert", None, ("dp", "tensor")),
            P("expert", None, ("dp", "tensor")),
            P("expert", ("dp", "tensor"), None),
        ),
        out_specs=(P(("expert", "tensor"), None), P(("expert", "tensor"), None)),
        check_vma=False,
    )
```

profile of v0, /device:TPU:2, one launch (start us, length us, event | category | flops | bytes accessed | tf_op | source)
XLA Modules:
  0.0 627.2 jit_solution(16614282896826630612)
XLA Ops:
  10.5 1.8 convolution_convert_fusion.1
  12.4 18.7 %all_to_all.20 = bf16[8,2,6144]{2,1,0:T(2,128)(2,1)S(1)} all-to-all(bf16[8,2,6144]{2,1,0:T(2,128)(2,1)S(1)} %reshape.232), channel_id=1, replica_groups=mesh['dp'=4,'expert'=8,'tensor'=8] {'expert'}, dimensions={0} | all-to-all | bytes 393216 | tf_op jit(solution)/shard_map/all_to_all | solution.py:75
  32.7 1.9 fusion.14
  34.6 1.9 fusion
  36.6 12.2 %all_to_all.21 = bf16[8,2,6144]{2,1,0:T(2,128)(2,1)S(1)} all-to-all(bf16[8,2,6144]{2,1,0:T(2,128)(2,1)S(1)} %reshape.236), channel_id=1, replica_groups=mesh['dp'=4,'expert'=8,'tensor'=8] {'expert'}, dimensions={0} | all-to-all | bytes 393216 | tf_op jit(solution)/shard_map/all_to_all | solution.py:76
  49.6 31.8 %all-gather.5.cloned.1.call-done = bf16[8,64,6144]{2,0,1:T(8,128)(2,1)} async-done(((bf16[8,2,6144]{2,0,1:T(8,128)(2,1)}), bf16[8,64,6144]{2,0,1:T(8,128)(2,1)}) %all-gather.5.cloned.1.call-update) | async-done | bytes 6291472 | tf_op jit(solution)/shard_map/all_gather | solution.py:80
  81.4 6.2 copy.28
  87.7 2.6 fusion.11
  90.3 2.6 fusion.7
  92.9 44.5 %all-gather.7.cloned.1.call-done = bf16[8,64,6144]{2,0,1:T(8,128)(2,1)} async-done(((bf16[8,2,6144]{2,0,1:T(8,128)(2,1)}), bf16[8,64,6144]{2,0,1:T(8,128)(2,1)}) %all-gather.7.cloned.1.call-update) | async-done | bytes 6291472 | tf_op jit(solution)/shard_map/all_gather | solution.py:80
  137.4 6.4 %copy.30 = bf16[8,64,6144]{2,1,0:T(8,128)(2,1)S(1)} copy(bf16[8,64,6144]{2,0,1:T(8,128)(2,1)} %all-gather.7.cloned.1.call-done) | data formatting | bytes 12582912 | tf_op jit(solution)/shard_map/all_gather | solution.py:80
  143.8 2.3 fusion.3
  146.2 6.5 %fusion.9 = f32[512,6144]{1,0:T(8,128)} fusion(bf16[1,6144,256]{2,1,0:T(8,128)(2,1)S(1)} %copy-done, f32[512,256]{1,0:T(8,128)S(1)} %copy-done.4, f32[512,256]{1,0:T(8,128)S(1)} %fusion.3, f32[512,256]{1,0:T(8,128)S(1)} %copy-done.9), kind=kOutput, calls=%fused_computation.23 | convolution fusion | flops 1611923456 | bytes 17301504 | tf_op jit(solution)/shard_map/dot_general | solution.py:121
  152.7 9.1 %add_convert_fusion = bf16[512,6144]{1,0:T(8,128)(2,1)} fusion(f32[512,6144]{1,0:T(8,128)} %fusion.9, bf16[1,6144,256]{2,1,0:T(8,128)(2,1)S(1)} %copy-done.8, f32[512,256]{1,0:T(8,128)S(1)} %fusion.3, f32[512,256]{1,0:T(8,128)S(1)} %copy-done.4), kind=kOutput, calls=%fused_computation.8 | convolution fusion | flops 1617690624 | bytes 23068672 | tf_op jit(solution)/shard_map/dot_general | solution.py:122
  161.7 7.1 %all-to-all-start.3 = ((bf16[8,64,6144]{2,1,0:T(8,128)(2,1)}), bf16[8,64,6144]{2,1,0:T(8,128)(2,1)}, u32[]{:S(2)}, u32[]{:S(2)}) async-start(bf16[8,64,6144]{2,1,0:T(8,128)(2,1)} %bitcast.62), calls=%async_computation.3 | async-start | bytes 12582912 | tf_op jit(solution)/shard_map/all_to_all | solution.py:100
  168.9 6.3 %convolution_convert_fusion = bf16[512,6144]{1,0:T(8,128)(2,1)} fusion(bf16[1,256,6144]{2,1,0:T(8,128)(2,1)} %param.13, f32[512,256]{1,0:T(8,128)S(1)} %copy-done.10, f32[512,256]{1,0:T(8,128)S(1)} %copy-done.5), kind=kOutput, calls=%fused_computation.9 | convolution fusion | flops 1614544896 | bytes 10485760 | tf_op jit(solution)/shard_map/dot_general | solution.py:117
  175.2 135.6 %all-to-all-done.3 = bf16[8,64,6144]{2,1,0:T(8,128)(2,1)} async-done(((bf16[8,64,6144]{2,1,0:T(8,128)(2,1)}), bf16[8,64,6144]{2,1,0:T(8,128)(2,1)}, u32[]{:S(2)}, u32[]{:S(2)}) %all-to-all-start.3) | async-done | bytes 6291488 | tf_op jit(solution)/shard_map/all_to_all | solution.py:100
  310.8 4.8 all-to-all-start.1
  315.7 1.2 gather_fusion
  316.9 1.2 gather_fusion.3
  318.2 1.5 gather_fusion.1
  319.7 1.7 gather_fusion.4
  321.4 6.6 %gather_fusion.6 = bf16[128,6144]{1,0:T(8,128)(2,1)S(1)} fusion(bf16[512,6144]{1,0:T(8,128)(2,1)} %bitcast.22, s32[1024]{0:T(1024)S(1)} %pad_clamp_fusion.1), kind=kCustom, calls=%fused_computation.6 | custom fusion | bytes 3146240 | tf_op jit(solution)/shard_map/gather | solution.py:103
  328.0 6.6 %gather_fusion.7 = bf16[128,6144]{1,0:T(8,128)(2,1)S(1)} fusion(bf16[512,6144]{1,0:T(8,128)(2,1)} %bitcast.22, s32[1024]{0:T(1024)S(1)} %pad_clamp_fusion), kind=kCustom, calls=%fused_computation.7 | custom fusion | bytes 3146240 | tf_op jit(solution)/shard_map/gather | solution.py:103
  334.6 122.8 %all-to-all-done.1 = bf16[8,64,6144]{2,1,0:T(8,128)(2,1)} async-done(((bf16[8,64,6144]{2,1,0:T(8,128)(2,1)}), bf16[8,64,6144]{2,1,0:T(8,128)(2,1)}, u32[]{:S(2)}, u32[]{:S(2)}) %all-to-all-start.1) | async-done | bytes 6291488 | tf_op jit(solution)/shard_map/all_to_all | solution.py:100
  457.4 7.7 %gather_fusion.2 = bf16[128,6144]{1,0:T(8,128)(2,1)} fusion(bf16[512,6144]{1,0:T(8,128)(2,1)} %bitcast.11, s32[1024]{0:T(1024)S(1)} %pad_clamp_fusion.1), kind=kCustom, calls=%fused_computation.2 | custom fusion | bytes 3146240 | tf_op jit(solution)/shard_map/gather | solution.py:103
  465.2 7.9 %gather_fusion.5 = bf16[128,6144]{1,0:T(8,128)(2,1)} fusion(bf16[512,6144]{1,0:T(8,128)(2,1)} %bitcast.11, s32[1024]{0:T(1024)S(1)} %pad_clamp_fusion), kind=kCustom, calls=%fused_computation.5 | custom fusion | bytes 3146240 | tf_op jit(solution)/shard_map/gather | solution.py:103
  473.1 1.6 add_convert_fusion.1
  475.6 1.9 add_convert_fusion.2
  478.7 112.7 %all-reduce.7.cloned.1.call-done = (bf16[128,6144]{1,0:T(8,128)(2,1)}, bf16[128,6144]{1,0:T(8,128)(2,1)}) async-done(((bf16[128,6144]{1,0:T(8,128)(2,1)}, bf16[128,6144]{1,0:T(8,128)(2,1)}), (bf16[128,6144]{1,0:T(8,128)(2,1)}, bf16[128,6144]{1,0:T(8,128)(2,1)})) %all-reduce.7.cloned.1.call-update) | async-done | bytes 3145744
  592.4 13.6 %all-gather = bf16[4,4,6144]{2,1,0:T(4,128)(2,1)S(1)} all-gather(bf16[1,4,6144]{2,1,0:T(4,128)(2,1)S(1)} %dynamic-slice_bitcast_fusion.1), channel_id=1, replica_groups=mesh['dp'=4,'expert'=8,'tensor'=8] {'dp'}, dimensions={0}, use_global_device_ids=true | all-gather | bytes 245760 | tf_op jit(solution)/shard_map/all_gather | solution.py:125
  607.6 12.1 %all-gather.1 = bf16[4,4,6144]{2,1,0:T(4,128)(2,1)S(1)} all-gather(bf16[1,4,6144]{2,1,0:T(4,128)(2,1)S(1)} %dynamic-slice_bitcast_fusion), channel_id=1, replica_groups=mesh['dp'=4,'expert'=8,'tensor'=8] {'dp'}, dimensions={0}, use_global_device_ids=true | all-gather | bytes 245760 | tf_op jit(solution)/shard_map/all_gather | solution.py:126
  (64 shorter events, 10.8 us)
Async XLA Ops:
  7.2 80.5 %copy-start = (bf16[1,6144,256]{2,1,0:T(8,128)(2,1)S(1)}, bf16[1,6144,256]{2,1,0:T(8,128)(2,1)}, u32[]{:S(2)}) copy-start(bf16[1,6144,256]{2,1,0:T(8,128)(2,1)} %param.11) | copy-start | bytes 9437188
  7.2 74.2 %all-gather.5.cloned.1.call-start = ((), (), s32[]{:S(2)}) async-start(), calls=%async_computation.4 | async-start | bytes 6488064 | tf_op jit(solution)/shard_map/all_gather | solution.py:80
  31.9 105.5 %all-gather.7.cloned.1.call-start = ((), (), s32[]{:S(2)}) async-start(), calls=%async_computation.5 | async-start | bytes 6488064 | tf_op jit(solution)/shard_map/all_gather | solution.py:80
  87.6 2.6 copy-start.7
  137.4 6.4 %copy-start.6 = (bf16[1,256,6144]{2,1,0:T(8,128)(2,1)S(1)}, bf16[1,256,6144]{2,1,0:T(8,128)(2,1)}, u32[]{:S(2)}) copy-start(bf16[1,256,6144]{2,1,0:T(8,128)(2,1)} %param.13) | copy-start | bytes 9437188
  143.8 2.4 copy-start.4
  143.8 2.4 copy-start.9
  146.2 6.5 %copy-start.8 = (bf16[1,6144,256]{2,1,0:T(8,128)(2,1)S(1)}, bf16[1,6144,256]{2,1,0:T(8,128)(2,1)}, u32[]{:S(2)}) copy-start(bf16[1,6144,256]{2,1,0:T(8,128)(2,1)} %param.12) | copy-start | bytes 9437188
  161.7 7.2 %copy-start.5 = (f32[512,256]{1,0:T(8,128)S(1)}, f32[512,256]{1,0:T(8,128)}, u32[]{:S(2)}) copy-start(f32[512,256]{1,0:T(8,128)} %fusion.11) | copy-start | bytes 1572868
  161.7 7.2 %copy-start.10 = (f32[512,256]{1,0:T(8,128)S(1)}, f32[512,256]{1,0:T(8,128)}, u32[]{:S(2)}) copy-start(f32[512,256]{1,0:T(8,128)} %fusion.7) | copy-start | bytes 1572868
  161.7 149.0 %all-to-all-start.3 = ((bf16[8,64,6144]{2,1,0:T(8,128)(2,1)}), bf16[8,64,6144]{2,1,0:T(8,128)(2,1)}, u32[]{:S(2)}, u32[]{:S(2)}) async-start(bf16[8,64,6144]{2,1,0:T(8,128)(2,1)} %bitcast.62), calls=%async_computation.3 | async-start | bytes 12582912 | tf_op jit(solution)/shard_map/all_to_all | solution.py:100
  310.8 146.6 %all-to-all-start.1 = ((bf16[8,64,6144]{2,1,0:T(8,128)(2,1)}), bf16[8,64,6144]{2,1,0:T(8,128)(2,1)}, u32[]{:S(2)}, u32[]{:S(2)}) async-start(bf16[8,64,6144]{2,1,0:T(8,128)(2,1)} %bitcast.61), calls=%async_computation.1 | async-start | bytes 12582912 | tf_op jit(solution)/shard_map/all_to_all | solution.py:100
  315.6 275.9 %all-reduce.7.cloned.1.call-start = ((), (), s32[]{:S(2)}) async-start(), calls=%async_computation.6 | async-start | bytes 6291456
  473.1 1.6 copy-start.2
  473.1 2.4 copy-start.3
  475.6 1.9 copy-start.11
  475.6 144.9 %copy-start.1 = (bf16[1,6144,256]{2,1,0:T(8,128)(2,1)S(1)}, bf16[1,6144,256]{2,1,0:T(8,128)(2,1)}, u32[]{:S(2)}) copy-start(bf16[1,6144,256]{2,1,0:T(8,128)(2,1)} %param.11) | copy-start | bytes 9437188
Sparse Core Ops, SparseCore 0:
  32.0 49.3 all-gather.4
  84.5 52.8 all-gather.6
  477.6 113.8 all-reduce.6
where the time goes:
time: 630 us; the launch traced here: 627 us
  waiting for transfers between devices  448 us (71%)
  blocking collectives  56.7 us (9%)
  local copies, waits for them, and re-layouts  55.3 us (9%)
  matrix products  34.9 us (6%)
  between operations  14.9 us (2%)
  starting transfers between devices  12 us (2%)
    all_to_all x2, waiting for transfers between devices, settle(): lax.all_to_all(shaped, 'expert', split_axis=0, concat_axis=0, tiled=True)  258 us
    unnamed x4, waiting for transfers between devices  113 us
    all_gather x2, waiting for transfers between devices, move_in(): piece = lax.all_gather(arrived, ('dp', 'tensor'), axis=1, tiled=True)  76.3 us
    all_to_all x1, blocking collectives, local(): lax.all_to_all(rows_fwd.reshape(shape), 'expert', split_axis=0, concat_ax...  18.7 us
    gather x2, local copies, waits for them, and re-layouts, settle(): back[slot_two].astype(jnp.float32)  14.5 us
    gather x2, local copies, waits for them, and re-layouts, settle(): back[slot_one].astype(jnp.float32)  14.3 us
    all_gather x1, blocking collectives, local(): lax.all_gather(out_piece, 'dp', axis=0, tiled=True)  13.6 us
    all_gather x2, local copies, waits for them, and re-layouts, move_in(): piece = lax.all_gather(arrived, ('dp', 'tensor'), axis=1, tiled=True)  12.6 us
  transfers between devices with their start and end apart: 5, of which 5 were waited for; matrix products, arithmetic and copies ran while one was open for 7% of the time, Pallas kernels for 0%

commit v1 on v0

--- a/solution.py
+++ b/solution.py
@@ -77,7 +77,15 @@
     )
 
     def move_in(arrived, project):
-        piece = lax.all_gather(arrived, ("dp", "tensor"), axis=1, tiled=True)
+        piece = jnp.concatenate(
+            lax.all_to_all(
+                jnp.stack([arrived for _ in range(lax.axis_size(("dp", "tensor")))]),
+                axis_name=("dp", "tensor"),
+                split_axis=0,
+                concat_axis=0,
+            ),
+            axis=1,
+        )
         result = project(piece.reshape(-1, width))
         spread = result.reshape(piece.shape[0], piece.shape[1], -1)
         return spread.reshape(-1, spread.shape[2])

time: 630 us -> 742 us (1.18)
  blocking collectives: 56.7 us -> 117 us
  local copies, waits for them, and re-layouts: 55.3 us -> 95.8 us
  starting transfers between devices: 12 us -> 25.3 us
    all_gather x2 -> x0, waiting for transfers between devices: 76.3 us -> none  [move_in(): piece = lax.all_gather(arrived, ('dp', 'tensor'), axis=1, tiled=True)]
    all_to_all x1, blocking collectives: 12.2 us -> 78.1 us  [move_in(): lax.all_to_all(jnp.stack([arrived for _ in range(lax.axis_size(('dp', 'te...]
    all_to_all x0 -> x2, waiting for transfers between devices: none -> 63.9 us  [the longest x1 56 us: move_in(): lax.all_to_all(jnp.stack([arrived for _ in range(lax.axis_size(('dp', 'te...]
    another operation x1 -> x5, local copies, waits for them, and re-layouts: 0.01 us -> 39.2 us  [the longest x2 26.6 us: move_in(): result = project(piece.reshape(-1, width))]
    all_to_all x0 -> x2, starting transfers between devices: none -> 15.6 us  [the longest x1 8.47 us: local(): lax.all_to_all(rows_bwd.reshape(shape), 'expert', split_axis=0, concat_ax...]
    reshape x0 -> x2, local copies, waits for them, and re-layouts: none -> 13.8 us  [move_in(): jnp.concatenate(lax.all_to_all(jnp.stack([arrived for _ in range(lax.axis...]
    all_gather x2 -> x0, local copies, waits for them, and re-layouts: 12.6 us -> none  [move_in(): piece = lax.all_gather(arrived, ('dp', 'tensor'), axis=1, tiled=True)]
    unnamed x4 -> x2, waiting for transfers between devices: 113 us -> 122 us
where the time goes in v1:
time: 742 us; the launch traced here: 740 us
  waiting for transfers between devices  443 us (60%)
  blocking collectives  117 us (16%)
  local copies, waits for them, and re-layouts  95.8 us (13%)
  matrix products  37.9 us (5%)
  starting transfers between devices  25.3 us (3%)
  between operations  15 us (2%)
    all_to_all x2, waiting for transfers between devices, settle(): lax.all_to_all(shaped, 'expert', split_axis=0, concat_axis=0, tiled=True)  258 us
    unnamed x2, waiting for transfers between devices  122 us
    all_to_all x1, blocking collectives, move_in(): lax.all_to_all(jnp.stack([arrived for _ in range(lax.axis_size(('dp', 'te...  78.1 us
    all_to_all x1, waiting for transfers between devices, move_in(): lax.all_to_all(jnp.stack([arrived for _ in range(lax.axis_size(('dp', 'te...  56 us
    another operation x2, local copies, waits for them, and re-layouts, move_in(): result = project(piece.reshape(-1, width))  26.6 us
  transfers between devices with their start and end apart: 5, of which 5 were waited for; matrix products, arithmetic and copies ran while one was open for 7% of the time, Pallas kernels for 0%

profile of v1, /device:TPU:2, one launch (start us, length us, event | category | flops | bytes accessed | tf_op | source)
XLA Modules:
  0.0 740.2 jit_solution(17582667050324831859)
XLA Ops:
  11.2 1.9 fusion.14
  13.1 1.9 fusion
  15.8 8.5 %all-to-all-start.3 = ((bf16[8,2,6144]{2,1,0:T(2,128)(2,1)}), bf16[8,2,6144]{2,1,0:T(2,128)(2,1)S(1)}, u32[]{:S(2)}, u32[]{:S(2)}) async-start(bf16[8,2,6144]{2,1,0:T(2,128)(2,1)} %reshape.240), calls=%async_computation.3 | async-start | bytes 393216 | tf_op jit(solution)/shard_map/all_to_all | solution.py:76
  26.9 7.8 %all-to-all-done.3 = bf16[8,2,6144]{2,1,0:T(2,128)(2,1)S(1)} async-done(((bf16[8,2,6144]{2,1,0:T(2,128)(2,1)}), bf16[8,2,6144]{2,1,0:T(2,128)(2,1)S(1)}, u32[]{:S(2)}, u32[]{:S(2)}) %all-to-all-start.3) | async-done | bytes 196640 | tf_op jit(solution)/shard_map/all_to_all | solution.py:76
  34.7 13.1 %all_to_all.30 = bf16[8,2,6144]{2,1,0:T(2,128)(2,1)S(1)} all-to-all(bf16[8,2,6144]{2,1,0:T(2,128)(2,1)} %reshape.236), channel_id=1, replica_groups=mesh['dp'=4,'expert'=8,'tensor'=8] {'expert'}, dimensions={0} | all-to-all | bytes 393216 | tf_op jit(solution)/shard_map/all_to_all | solution.py:75
  47.8 6.0 stack.5
  53.8 78.1 %all_to_all.31 = bf16[32,8,2,6144]{3,2,1,0:T(2,128)(2,1)} all-to-all(bf16[32,8,2,6144]{3,2,1,0:T(2,128)(2,1)S(1)} %stack.5), channel_id=1, replica_groups=mesh['dp'=4,'expert'=8,'tensor'=8] {'dp','tensor'}, dimensions={0} | all-to-all | bytes 12582912 | tf_op jit(solution)/shard_map/all_to_all | solution.py:81
  131.9 6.6 stack.4
  138.5 7.1 all-to-all-start.1
  145.7 6.8 copy.16
  152.5 13.3 %reshape_reshape.7 = bf16[512,6144]{1,0:T(8,128)(2,1)} reshape(bf16[8,32,2,6144]{3,2,1,0:T(2,128)(2,1)} %copy.16) | data formatting | bytes 12582912 | tf_op jit(solution)/shard_map/reshape;reshape | solution.py:89
  165.8 56.0 %all-to-all-done.1 = bf16[32,8,2,6144]{3,2,1,0:T(2,128)(2,1)} async-done(((bf16[32,8,2,6144]{3,2,1,0:T(2,128)(2,1)}), bf16[32,8,2,6144]{3,2,1,0:T(2,128)(2,1)}, u32[]{:S(2)}, u32[]{:S(2)}) %all-to-all-start.1) | async-done | bytes 6291488 | tf_op jit(solution)/shard_map/all_to_all | solution.py:81
  221.8 6.9 copy.15
  228.8 13.3 %reshape_reshape.6 = bf16[512,6144]{1,0:T(8,128)(2,1)} reshape(bf16[8,32,2,6144]{3,2,1,0:T(2,128)(2,1)} %copy.15) | data formatting | bytes 12582912 | tf_op jit(solution)/shard_map/reshape;reshape | solution.py:89
  242.1 4.7 fusion.11
  246.8 4.0 fusion.7
  250.9 1.8 fusion.3
  252.8 6.5 fusion.9
  259.2 9.0 %add_convert_fusion = bf16[512,6144]{1,0:T(8,128)(2,1)} fusion(f32[512,6144]{1,0:T(8,128)} %fusion.9, bf16[1,6144,256]{2,1,0:T(8,128)(2,1)S(1)} %copy-done.8, f32[512,256]{1,0:T(8,128)S(1)} %fusion.3, f32[512,256]{1,0:T(8,128)S(1)} %fusion.11), kind=kOutput, calls=%fused_computation.8 | convolution fusion | flops 1617690624 | bytes 23068672 | tf_op jit(solution)/shard_map/dot_general | solution.py:130
  268.3 4.9 all-to-all-start.5
  273.2 6.3 convolution_convert_fusion
  279.5 135.0 %all-to-all-done.5 = bf16[8,64,6144]{2,1,0:T(8,128)(2,1)} async-done(((bf16[8,64,6144]{2,1,0:T(8,128)(2,1)}), bf16[8,64,6144]{2,1,0:T(8,128)(2,1)}, u32[]{:S(2)}, u32[]{:S(2)}) %all-to-all-start.5) | async-done | bytes 6291488 | tf_op jit(solution)/shard_map/all_to_all | solution.py:108
  414.5 4.8 all-to-all-start.2
  425.2 6.6 gather_fusion.6
  431.8 6.6 gather_fusion.7
  438.4 122.8 %all-to-all-done.2 = bf16[8,64,6144]{2,1,0:T(8,128)(2,1)} async-done(((bf16[8,64,6144]{2,1,0:T(8,128)(2,1)}), bf16[8,64,6144]{2,1,0:T(8,128)(2,1)}, u32[]{:S(2)}, u32[]{:S(2)}) %all-to-all-start.2) | async-done | bytes 6291488 | tf_op jit(solution)/shard_map/all_to_all | solution.py:108
  561.2 7.8 %gather_fusion.2 = bf16[128,6144]{1,0:T(8,128)(2,1)} fusion(bf16[512,6144]{1,0:T(8,128)(2,1)} %bitcast.11, s32[1024]{0:T(1024)S(1)} %pad_clamp_fusion.1), kind=kCustom, calls=%fused_computation.2 | custom fusion | bytes 3146240 | tf_op jit(solution)/shard_map/gather | solution.py:111
  568.9 8.0 %gather_fusion.5 = bf16[128,6144]{1,0:T(8,128)(2,1)} fusion(bf16[512,6144]{1,0:T(8,128)(2,1)} %bitcast.11, s32[1024]{0:T(1024)S(1)} %pad_clamp_fusion), kind=kCustom, calls=%fused_computation.5 | custom fusion | bytes 3146240 | tf_op jit(solution)/shard_map/gather | solution.py:111
  579.4 1.9 add_convert_fusion.2
  582.5 121.8 %all-reduce.7.cloned.1.call-done = (bf16[128,6144]{1,0:T(8,128)(2,1)}, bf16[128,6144]{1,0:T(8,128)(2,1)}) async-done(((bf16[128,6144]{1,0:T(8,128)(2,1)}, bf16[128,6144]{1,0:T(8,128)(2,1)}), (bf16[128,6144]{1,0:T(8,128)(2,1)}, bf16[128,6144]{1,0:T(8,128)(2,1)})) %all-reduce.7.cloned.1.call-update) | async-done | bytes 3145744
  705.2 13.6 %all-gather = bf16[4,4,6144]{2,1,0:T(4,128)(2,1)S(1)} all-gather(bf16[1,4,6144]{2,1,0:T(4,128)(2,1)S(1)} %dynamic-slice_bitcast_fusion.1), channel_id=1, replica_groups=mesh['dp'=4,'expert'=8,'tensor'=8] {'dp'}, dimensions={0}, use_global_device_ids=true | all-gather | bytes 245760 | tf_op jit(solution)/shard_map/all_gather | solution.py:133
  720.5 12.1 %all-gather.1 = bf16[4,4,6144]{2,1,0:T(4,128)(2,1)S(1)} all-gather(bf16[1,4,6144]{2,1,0:T(4,128)(2,1)S(1)} %dynamic-slice_bitcast_fusion), channel_id=1, replica_groups=mesh['dp'=4,'expert'=8,'tensor'=8] {'dp'}, dimensions={0}, use_global_device_ids=true | all-gather | bytes 245760 | tf_op jit(solution)/shard_map/all_gather | solution.py:134
  (73 shorter events, 19.6 us)
Async XLA Ops:
  7.2 234.9 %copy-start = (bf16[1,6144,256]{2,1,0:T(8,128)(2,1)S(1)}, bf16[1,6144,256]{2,1,0:T(8,128)(2,1)}, u32[]{:S(2)}) copy-start(bf16[1,6144,256]{2,1,0:T(8,128)(2,1)} %param.11) | copy-start | bytes 9437188
  10.3 5.5 copy-start.11
  10.3 5.5 copy-start.12
  15.8 18.9 %all-to-all-start.3 = ((bf16[8,2,6144]{2,1,0:T(2,128)(2,1)}), bf16[8,2,6144]{2,1,0:T(2,128)(2,1)S(1)}, u32[]{:S(2)}, u32[]{:S(2)}) async-start(bf16[8,2,6144]{2,1,0:T(2,128)(2,1)} %reshape.240), calls=%async_computation.3 | async-start | bytes 393216 | tf_op jit(solution)/shard_map/all_to_all | solution.py:76
  138.5 83.3 %all-to-all-start.1 = ((bf16[32,8,2,6144]{3,2,1,0:T(2,128)(2,1)}), bf16[32,8,2,6144]{3,2,1,0:T(2,128)(2,1)}, u32[]{:S(2)}, u32[]{:S(2)}) async-start(bf16[32,8,2,6144]{3,2,1,0:T(2,128)(2,1)} %stack.4), calls=%async_computation.1 | async-start | bytes 12582912 | tf_op jit(solution)/shard_map/all_to_all | solution.py:81
  242.1 4.7 copy-start.2
  242.1 8.8 %slice-start = ((s8[6291456]{0:T(1024)(128)(4,1)}), s8[4194304]{0:T(1024)(128)(4,1)S(1)}, s32[]{:S(2)}) async-start(s8[6291456]{0:T(1024)(128)(4,1)} %bitcast.64), calls=%async_computation.7 | async-start | bytes 8388608
  246.8 12.4 %copy-start.5 = (f32[512,256]{1,0:T(8,128)}, f32[512,256]{1,0:T(8,128)S(1)}, u32[]{:S(2)}) copy-start(f32[512,256]{1,0:T(8,128)S(1)} %fusion.11) | copy-start | bytes 1572868
  246.8 4.0 slice-start.1
  246.8 4.0 copy-start.7
  250.9 1.8 copy-start.9
  252.7 6.5 copy-start.8
  268.3 4.9 copy-start.6
  268.3 4.9 copy-start.10
  268.3 146.3 %all-to-all-start.5 = ((bf16[8,64,6144]{2,1,0:T(8,128)(2,1)}), bf16[8,64,6144]{2,1,0:T(8,128)(2,1)}, u32[]{:S(2)}, u32[]{:S(2)}) async-start(bf16[8,64,6144]{2,1,0:T(8,128)(2,1)} %bitcast.63), calls=%async_computation.5 | async-start | bytes 12582912 | tf_op jit(solution)/shard_map/all_to_all | solution.py:108
  414.5 146.6 %all-to-all-start.2 = ((bf16[8,64,6144]{2,1,0:T(8,128)(2,1)}), bf16[8,64,6144]{2,1,0:T(8,128)(2,1)}, u32[]{:S(2)}, u32[]{:S(2)}) async-start(bf16[8,64,6144]{2,1,0:T(8,128)(2,1)} %bitcast.61), calls=%async_computation.2 | async-start | bytes 12582912 | tf_op jit(solution)/shard_map/all_to_all | solution.py:108
  419.3 285.0 %all-reduce.7.cloned.1.call-start = ((), (), s32[]{:S(2)}) async-start(), calls=%async_computation.6 | async-start | bytes 6291456
  576.9 1.6 copy-start.3
  576.9 2.4 copy-start.4
  579.3 1.9 copy-start.13
  579.4 154.0 %copy-start.1 = (bf16[1,6144,256]{2,1,0:T(8,128)(2,1)S(1)}, bf16[1,6144,256]{2,1,0:T(8,128)(2,1)}, u32[]{:S(2)}) copy-start(bf16[1,6144,256]{2,1,0:T(8,128)(2,1)} %param.11) | copy-start | bytes 9437188
Sparse Core Ops, SparseCore 0:
  581.4 122.8 all-reduce.6
